TPU v7x, 32 devices: a whole 2x2x4 slice. The times are simulated.
32 devices in a mesh: rows: 4 (over y, x), cols: 8 (over z, core).
Axes of the slice: x: 2, y: 2, z: 4, core: 2. Of those that a mesh axis runs over, the one named last changes fastest.
Arguments:
- images: bfloat16 [2, 64, 256, 1024], P(None, None, 'rows', 'cols'), may hold values from -6 to 6
- first_weight: bfloat16 [9, 64, 64], replicated, may hold values from -0.25 to 0.25
- second_weight: bfloat16 [9, 64, 64], replicated, may hold values from -0.25 to 0.25
- search_ranges: int32 [2, 32, 8], P(None, 'rows', 'cols'), may hold values from 0 to 16, as said below
Outputs:
- matched: bfloat16 [64, 256, 1024], P(None, 'rows', 'cols')
- disparity: float32 [256, 1024], P('rows', 'cols')
Inputs may be any that keep to these rules, and one draw needn't show every extreme that they name: search_ranges[0] is 0 to 1 and search_ranges[1] is 1 to 16; some block has search_ranges[0] = 1 together with search_ranges[1] = 16.
All inputs are finite; a program needn't handle non-finite values.
Results may differ from a plain program's by a relative error of at most 0.008.
Values may be sent and summed in bfloat16 or wider, within the bound.
No kernel may reach another device: no remote copies, remote signals or barrier semaphores. Data moves between devices by JAX's collectives and lax.ppermute only.
A program may use at most 128 MiB of HBM per device.

v0:
```python
import jax
import jax.numpy as jnp
from jax import lax
from jax.sharding import PartitionSpec as P

RG = 8
FIRST_DILATION = 2
SECOND_DILATION = 4
HOPS = 18
sharpness_divisor = 10.0
epsilon = 1e-05


def with_halo(block, sides, width):
    for axis, dim in sides:
        count = lax.axis_size(axis)
        forward = [(i, i + 1) for i in range(count - 1)]
        backward = [(target, source) for source, target in forward]
        low = lax.ppermute(
            lax.slice_in_dim(block, block.shape[dim] - width, None, axis=dim), axis, forward
        )
        high = lax.ppermute(lax.slice_in_dim(block, 0, width, axis=dim), axis, backward)
        block = jnp.concatenate([low, block, high], axis=dim)
    return block


def convolution_layer(images, weights, dilation):
    padded = with_halo(images, (("rows", 2), ("cols", 3)), dilation)
    height = images.shape[2]
    full_width = images.shape[3]
    summed = jnp.zeros((images.shape[0], weights.shape[1], height, full_width), jnp.float32)
    for row_tap in range(3):
        for horizontal_offset in range(3):
            window = padded[
                :,
                :,
                row_tap * dilation : row_tap * dilation + height,
                horizontal_offset * dilation : horizontal_offset * dilation + full_width,
            ]
            summed = summed + jnp.einsum(
                "oc,nchw->nohw",
                weights[3 * row_tap + horizontal_offset],
                window,
                preferred_element_type=jnp.float32,
            )
    return summed


def normalize(feature_maps):
    widened = feature_maps.astype(jnp.float32)
    return (
        widened * lax.rsqrt(jnp.mean(widened * widened, axis=1, keepdims=True) + epsilon)
    ).astype(jnp.bfloat16)


def hop_terms(source_descriptors, key_feats, hop_index, low_edge, high_edge):
    plane_total = source_descriptors.shape[0]
    segment = source_descriptors.shape[2]
    pairing_similarity = jnp.einsum(
        "cri,crm->rim", source_descriptors, key_feats, preferred_element_type=jnp.float32
    ) * (sharpness_divisor / plane_total)
    offsets = (
        hop_index * segment
        + lax.broadcasted_iota(jnp.int32, (segment, segment), 0)
        - lax.broadcasted_iota(jnp.int32, (segment, segment), 1)
    )
    inside = (offsets[None] >= low_edge[:, None, None]) & (offsets[None] < high_edge[:, None, None])
    rounded = jnp.where(inside, jnp.exp(pairing_similarity), 0.0).astype(jnp.bfloat16)
    norm_sum = jnp.sum(rounded, axis=-1, dtype=jnp.float32)
    shift_sum = jnp.sum(rounded * offsets.astype(jnp.float32)[None], axis=-1)
    feature_sum = jnp.einsum("rim,crm->cri", rounded, key_feats, preferred_element_type=jnp.float32)
    return (norm_sum, shift_sum, feature_sum)


def per_device(images, first_weight, second_weight, search_ranges):
    inner_activations = jax.nn.silu(convolution_layer(images, first_weight, FIRST_DILATION)).astype(
        jnp.bfloat16
    )
    feature_maps = (
        images.astype(jnp.float32)
        + convolution_layer(inner_activations, second_weight, SECOND_DILATION)
    ).astype(jnp.bfloat16)
    unit_feats = normalize(feature_maps)
    plane_total = unit_feats.shape[1]
    count_rows = unit_feats.shape[2]
    segment = unit_feats.shape[3]
    peer_count = lax.axis_size("cols")
    column = lax.axis_index("cols")
    band_rows = count_rows // peer_count
    full_width = segment * peer_count
    whole_rows = lax.all_to_all(unit_feats, "cols", split_axis=2, concat_axis=3, tiled=True)
    gathered = lax.all_gather(search_ranges, "cols", axis=2, tiled=True)
    spread_rows = jnp.repeat(gathered, RG, axis=1)
    own_ranges = lax.dynamic_slice_in_dim(spread_rows, column * band_rows, band_rows, 1).reshape(
        2, band_rows * peer_count
    )
    low_edge = segment * own_ranges[0]
    high_edge = segment * (own_ranges[0] + own_ranges[1])
    source_descriptors = whole_rows[0].reshape(plane_total, band_rows * peer_count, segment)
    padded = jnp.pad(whole_rows[1], ((0, 0), (0, 0), ((HOPS - 1) * segment, 0)))

    def accumulate(hop_index, carried):
        norm_sum, shift_sum, feature_sum = carried
        key_feats = lax.dynamic_slice_in_dim(
            padded, (HOPS - 1 - hop_index) * segment, full_width, 2
        )
        key_feats = key_feats.reshape(plane_total, band_rows * peer_count, segment)
        new_terms = hop_terms(source_descriptors, key_feats, hop_index, low_edge, high_edge)
        return (norm_sum + new_terms[0], shift_sum + new_terms[1], feature_sum + new_terms[2])

    zero_rows = jnp.zeros((band_rows * peer_count, segment), jnp.float32)
    zero_feats = jnp.zeros((plane_total, band_rows * peer_count, segment), jnp.float32)
    norm_sum, shift_sum, feature_sum = lax.fori_loop(
        0, HOPS, accumulate, (zero_rows, zero_rows, zero_feats)
    )
    matched_rows = (
        (feature_sum / norm_sum[None])
        .astype(jnp.bfloat16)
        .reshape(plane_total, band_rows, full_width)
    )
    disparity_rows = (shift_sum / norm_sum / segment).reshape(band_rows, full_width)
    matched = lax.all_to_all(matched_rows, "cols", split_axis=2, concat_axis=1, tiled=True)
    disparity = lax.all_to_all(disparity_rows, "cols", split_axis=1, concat_axis=0, tiled=True)
    return (matched, disparity)


def solution(mesh):
    placed = (P(None, None, "rows", "cols"), P(), P(), P(None, "rows", "cols"))
    return jax.shard_map(
        per_device,
        mesh=mesh,
        in_specs=placed,
        out_specs=(P(None, "rows", "cols"), P("rows", "cols")),
        check_vma=False,
    )
```

profile of v0, /device:TPU:4, one launch (start us, length us, event | category | flops | bytes accessed | tf_op | source)
XLA Modules:
  0.0 488.2 jit_solution(17448177616877431964)
XLA Ops:
  3.8 3.4 collective-permute-start
  7.2 3.3 collective-permute-start.1
  10.6 3.7 fusion.64
  15.7 3.2 fusion.101
  19.0 3.7 copy.72
  24.0 3.7 copy.69
  27.7 3.2 collective-permute-start.2
  30.9 4.3 fusion.44
  37.8 4.8 copy.70
  42.7 4.9 fusion.19
  50.7 4.6 copy.73
  55.2 5.3 %fusion.16 = f32[2,64,128,64]{2,3,1,0:T(8,128)} fusion(bf16[2,64,68,128]{3,1,2,0:T(8,128)(2,1)S(1)} %constant_dynamic-update-slice_fusion, bf16[2,64,68,2]{3,1,2,0:T(8,128)(2,1)} %copy.73, bf16[9,64,64]{2,1,0:T(8,128)(2,1)S(1)} %copy-done.13), kind=kOutput, calls=%fused_computation.40 | convolution fusion | flops 138412032 | bytes 6473728 | tf_op jit(solution)/shard_map/oc,nchw->nohw/dot_general | solution.py:40
  60.5 3.5 fusion.13
  64.0 3.2 fusion.46
  67.2 12.5 %fusion.11 = bf16[2,64,64,128]{3,1,2,0:T(8,128)(2,1)S(1)} fusion(f32[2,64,128,64]{2,3,1,0:T(8,128)} %fusion.44, f32[2,64,128,64]{2,3,1,0:T(8,128)} %fusion.46, f32[2,64,128,64]{2,3,1,0:T(8,128)} %fusion.13, f32[2,64,128,64]{2,3,1,0:T(8,128)} %fusion.64, f32[2,64,128,64]{2,3,1,0:T(8,128)} %fusion.19, f32[2,64,128,64]{2,3,1,0:T(8,128)} %fusion.16, ...), kind=kOutput, calls=%fused_computation.35 | convolution fusion | flops 152043520 | bytes 40124416 | tf_op jit(solution)/shard_map/oc,nchw->nohw/dot_general | solution.py:40
  82.2 16.4 %collective-permute-start.5 = (bf16[2,64,4,128]{3,1,2,0:T(8,128)(2,1)S(1)}, bf16[2,64,4,128]{3,1,2,0:T(8,128)(2,1)S(1)}, u32[]{:S(2)}, u32[]{:S(2)}) collective-permute-start(bf16[2,64,4,128]{3,1,2,0:T(8,128)(2,1)S(1)} %get-tuple-element.205), channel_id=1, source_target_pairs={{8,0},{16,8},{24,16},{9,1},{17,9},{25,17},{10,2},{18,10},{26,18},{... | collective-permute-start | bytes 393224 | tf_op jit(solution)/shard_map/ppermute | solution.py:22
  101.7 3.3 fusion.100
  105.0 4.2 copy.76
  111.7 4.0 copy.78
  122.4 4.7 copy.77
  127.2 4.8 copy.79
  132.0 5.9 %pad_maximum_fusion = (bf16[2,64,72,132]{3,1,2,0:T(8,128)(2,1)S(1)}, bf16[2,64,72,132]{3,1,2,0:T(8,128)(2,1)S(1)}) fusion(bf16[2,64,72,4]{3,1,2,0:T(8,128)(2,1)} %copy.79, bf16[2,64,4,128]{3,1,2,0:T(8,128)(2,1)S(1)} %collective-permute-done.5, bf16[2,64,64,128]{3,1,2,0:T(8,128)(2,1)S(1)} %copy-done.1, bf16[2,64,4,128]{3,1,2,0:T(8,128)(2,1)S(1)} %collective-permute-done.4, ...), kind=kLoop, calls=%fused_computation.25 | loop fusion | flops 19464192 | bytes 7372800 | tf_op jit(solution)/shard_map/concatenate | solution.py:23
  153.8 15.0 %fusion.5 = (f32[2,64,128]{2,1,0:T(8,128)S(1)}, bf16[2,64,64,128]{3,1,2,0:T(8,128)(2,1)}) fusion(bf16[2,64,72,132]{3,1,2,0:T(8,128)(2,1)} %copy-done.9, bf16[9,64,64]{2,1,0:T(8,128)(2,1)S(1)} %copy-done.14, f32[2,64,128,64]{2,3,1,0:T(8,128)} %fusion.28, f32[2,64,128,64]{2,3,1,0:T(8,128)} %fusion.30, f32[2,64,128,64]{2,3,1,0:T(8,128)} %fusion.32, ...), kind=kOutput, calls=%fused_computation.26 | convolution fusion | flops 148881408 | bytes 39927808 | tf_op jit(solution)/shard_map/oc,nchw->nohw/dot_general | solution.py:40
  172.7 6.6 %all-to-all-start = ((bf16[2,64,64,128]{3,1,0,2:T(8,128)(2,1)}), bf16[2,64,64,128]{3,1,0,2:T(8,128)(2,1)S(1)}, u32[]{:S(2)}, u32[]{:S(2)}) async-start(bf16[2,64,64,128]{3,1,0,2:T(8,128)(2,1)} %copy.80), calls=%async_computation | async-start | bytes 4194304 | tf_op jit(solution)/shard_map/all_to_all | solution.py:91
  179.4 41.5 %all_gather.3 = s32[2,8,8]{1,0,2:T(2,128)S(1)} all-gather(s32[2,8,1]{1,0,2:T(2,128)S(1)} %bitcast.188), channel_id=1, replica_groups=mesh['rows'=4,'cols'=8] {'cols'}, dimensions={2}, use_global_device_ids=true | all-gather | bytes 576 | tf_op jit(solution)/shard_map/all_gather | solution.py:92
  221.1 7.3 %all-to-all-done = bf16[2,64,64,128]{3,1,0,2:T(8,128)(2,1)S(1)} async-done(((bf16[2,64,64,128]{3,1,0,2:T(8,128)(2,1)}), bf16[2,64,64,128]{3,1,0,2:T(8,128)(2,1)S(1)}, u32[]{:S(2)}, u32[]{:S(2)}) %all-to-all-start) | async-done | bytes 2097184 | tf_op jit(solution)/shard_map/all_to_all | solution.py:91
  232.2 204.3 %while.18 = (s32[]{:T(128)}, f32[64,128]{1,0:T(8,128)S(1)}, f32[64,128]{1,0:T(8,128)S(1)}, f32[64,64,128]{2,0,1:T(8,128)}, s32[64]{0:T(128)S(1)}, /*index=5*/s32...) while((s32[]{:T(128)}, f32[64,128]{1,0:T(8,128)S(1)}, ...), condition=%wide.region_4.5_spmd.clone, body=%wide.region_1.4_spmd.clone.sunk | while | flops 280019072 | bytes 33031948 | solution.py:113
  234.1 5.1 %fusion.117 = (f32[64,128]{1,0:T(8,128)S(1)}, f32[64,128]{1,0:T(8,128)S(1)}, bf16[64,128,128]{1,2,0:T(8,128)(2,1)}) fusion(f32[128,128]{0,1:T(8,128)S(1)} %get-tuple-element.268, bf16[64,64,128]{2,0,1:T(8,128)(2,1)} %get-tuple-element.308, bf16[64,64,128]{2,1,0:T(8,128)(2,1)S(1)} %reshape.96, s32[64]{0:T(128)S(1)} %get-tuple-element.306, ...), kind=kOutput, calls=%fused_computation.2.clone.1 | convolution fusion | flops 144687104 | bytes 4391424 | tf_op jit(solution)/shard_map/while/body/eval_jaxpr/cri,crm->rim/dot_general | solution.py:59
  245.4 5.1 %fusion.117 = (f32[64,128]{1,0:T(8,128)S(1)}, f32[64,128]{1,0:T(8,128)S(1)}, bf16[64,128,128]{1,2,0:T(8,128)(2,1)}) fusion(f32[128,128]{0,1:T(8,128)S(1)} %get-tuple-element.268, bf16[64,64,128]{2,0,1:T(8,128)(2,1)} %get-tuple-element.308, bf16[64,64,128]{2,1,0:T(8,128)(2,1)S(1)} %reshape.96, s32[64]{0:T(128)S(1)} %get-tuple-element.306, ...), kind=kOutput, calls=%fused_computation.2.clone.1 | convolution fusion | flops 144687104 | bytes 4391424 | tf_op jit(solution)/shard_map/while/body/eval_jaxpr/cri,crm->rim/dot_general | solution.py:59
  256.8 5.1 %fusion.117 = (f32[64,128]{1,0:T(8,128)S(1)}, f32[64,128]{1,0:T(8,128)S(1)}, bf16[64,128,128]{1,2,0:T(8,128)(2,1)}) fusion(f32[128,128]{0,1:T(8,128)S(1)} %get-tuple-element.268, bf16[64,64,128]{2,0,1:T(8,128)(2,1)} %get-tuple-element.308, bf16[64,64,128]{2,1,0:T(8,128)(2,1)S(1)} %reshape.96, s32[64]{0:T(128)S(1)} %get-tuple-element.306, ...), kind=kOutput, calls=%fused_computation.2.clone.1 | convolution fusion | flops 144687104 | bytes 4391424 | tf_op jit(solution)/shard_map/while/body/eval_jaxpr/cri,crm->rim/dot_general | solution.py:59
  268.1 5.1 %fusion.117 = (f32[64,128]{1,0:T(8,128)S(1)}, f32[64,128]{1,0:T(8,128)S(1)}, bf16[64,128,128]{1,2,0:T(8,128)(2,1)}) fusion(f32[128,128]{0,1:T(8,128)S(1)} %get-tuple-element.268, bf16[64,64,128]{2,0,1:T(8,128)(2,1)} %get-tuple-element.308, bf16[64,64,128]{2,1,0:T(8,128)(2,1)S(1)} %reshape.96, s32[64]{0:T(128)S(1)} %get-tuple-element.306, ...), kind=kOutput, calls=%fused_computation.2.clone.1 | convolution fusion | flops 144687104 | bytes 4391424 | tf_op jit(solution)/shard_map/while/body/eval_jaxpr/cri,crm->rim/dot_general | solution.py:59
  279.5 5.1 %fusion.117 = (f32[64,128]{1,0:T(8,128)S(1)}, f32[64,128]{1,0:T(8,128)S(1)}, bf16[64,128,128]{1,2,0:T(8,128)(2,1)}) fusion(f32[128,128]{0,1:T(8,128)S(1)} %get-tuple-element.268, bf16[64,64,128]{2,0,1:T(8,128)(2,1)} %get-tuple-element.308, bf16[64,64,128]{2,1,0:T(8,128)(2,1)S(1)} %reshape.96, s32[64]{0:T(128)S(1)} %get-tuple-element.306, ...), kind=kOutput, calls=%fused_computation.2.clone.1 | convolution fusion | flops 144687104 | bytes 4391424 | tf_op jit(solution)/shard_map/while/body/eval_jaxpr/cri,crm->rim/dot_general | solution.py:59
  290.8 5.1 %fusion.117 = (f32[64,128]{1,0:T(8,128)S(1)}, f32[64,128]{1,0:T(8,128)S(1)}, bf16[64,128,128]{1,2,0:T(8,128)(2,1)}) fusion(f32[128,128]{0,1:T(8,128)S(1)} %get-tuple-element.268, bf16[64,64,128]{2,0,1:T(8,128)(2,1)} %get-tuple-element.308, bf16[64,64,128]{2,1,0:T(8,128)(2,1)S(1)} %reshape.96, s32[64]{0:T(128)S(1)} %get-tuple-element.306, ...), kind=kOutput, calls=%fused_computation.2.clone.1 | convolution fusion | flops 144687104 | bytes 4391424 | tf_op jit(solution)/shard_map/while/body/eval_jaxpr/cri,crm->rim/dot_general | solution.py:59
  302.2 5.1 %fusion.117 = (f32[64,128]{1,0:T(8,128)S(1)}, f32[64,128]{1,0:T(8,128)S(1)}, bf16[64,128,128]{1,2,0:T(8,128)(2,1)}) fusion(f32[128,128]{0,1:T(8,128)S(1)} %get-tuple-element.268, bf16[64,64,128]{2,0,1:T(8,128)(2,1)} %get-tuple-element.308, bf16[64,64,128]{2,1,0:T(8,128)(2,1)S(1)} %reshape.96, s32[64]{0:T(128)S(1)} %get-tuple-element.306, ...), kind=kOutput, calls=%fused_computation.2.clone.1 | convolution fusion | flops 144687104 | bytes 4391424 | tf_op jit(solution)/shard_map/while/body/eval_jaxpr/cri,crm->rim/dot_general | solution.py:59
  313.5 5.1 %fusion.117 = (f32[64,128]{1,0:T(8,128)S(1)}, f32[64,128]{1,0:T(8,128)S(1)}, bf16[64,128,128]{1,2,0:T(8,128)(2,1)}) fusion(f32[128,128]{0,1:T(8,128)S(1)} %get-tuple-element.268, bf16[64,64,128]{2,0,1:T(8,128)(2,1)} %get-tuple-element.308, bf16[64,64,128]{2,1,0:T(8,128)(2,1)S(1)} %reshape.96, s32[64]{0:T(128)S(1)} %get-tuple-element.306, ...), kind=kOutput, calls=%fused_computation.2.clone.1 | convolution fusion | flops 144687104 | bytes 4391424 | tf_op jit(solution)/shard_map/while/body/eval_jaxpr/cri,crm->rim/dot_general | solution.py:59
  324.9 5.1 %fusion.117 = (f32[64,128]{1,0:T(8,128)S(1)}, f32[64,128]{1,0:T(8,128)S(1)}, bf16[64,128,128]{1,2,0:T(8,128)(2,1)}) fusion(f32[128,128]{0,1:T(8,128)S(1)} %get-tuple-element.268, bf16[64,64,128]{2,0,1:T(8,128)(2,1)} %get-tuple-element.308, bf16[64,64,128]{2,1,0:T(8,128)(2,1)S(1)} %reshape.96, s32[64]{0:T(128)S(1)} %get-tuple-element.306, ...), kind=kOutput, calls=%fused_computation.2.clone.1 | convolution fusion | flops 144687104 | bytes 4391424 | tf_op jit(solution)/shard_map/while/body/eval_jaxpr/cri,crm->rim/dot_general | solution.py:59
  336.2 5.1 %fusion.117 = (f32[64,128]{1,0:T(8,128)S(1)}, f32[64,128]{1,0:T(8,128)S(1)}, bf16[64,128,128]{1,2,0:T(8,128)(2,1)}) fusion(f32[128,128]{0,1:T(8,128)S(1)} %get-tuple-element.268, bf16[64,64,128]{2,0,1:T(8,128)(2,1)} %get-tuple-element.308, bf16[64,64,128]{2,1,0:T(8,128)(2,1)S(1)} %reshape.96, s32[64]{0:T(128)S(1)} %get-tuple-element.306, ...), kind=kOutput, calls=%fused_computation.2.clone.1 | convolution fusion | flops 144687104 | bytes 4391424 | tf_op jit(solution)/shard_map/while/body/eval_jaxpr/cri,crm->rim/dot_general | solution.py:59
  347.6 5.1 %fusion.117 = (f32[64,128]{1,0:T(8,128)S(1)}, f32[64,128]{1,0:T(8,128)S(1)}, bf16[64,128,128]{1,2,0:T(8,128)(2,1)}) fusion(f32[128,128]{0,1:T(8,128)S(1)} %get-tuple-element.268, bf16[64,64,128]{2,0,1:T(8,128)(2,1)} %get-tuple-element.308, bf16[64,64,128]{2,1,0:T(8,128)(2,1)S(1)} %reshape.96, s32[64]{0:T(128)S(1)} %get-tuple-element.306, ...), kind=kOutput, calls=%fused_computation.2.clone.1 | convolution fusion | flops 144687104 | bytes 4391424 | tf_op jit(solution)/shard_map/while/body/eval_jaxpr/cri,crm->rim/dot_general | solution.py:59
  358.9 5.1 %fusion.117 = (f32[64,128]{1,0:T(8,128)S(1)}, f32[64,128]{1,0:T(8,128)S(1)}, bf16[64,128,128]{1,2,0:T(8,128)(2,1)}) fusion(f32[128,128]{0,1:T(8,128)S(1)} %get-tuple-element.268, bf16[64,64,128]{2,0,1:T(8,128)(2,1)} %get-tuple-element.308, bf16[64,64,128]{2,1,0:T(8,128)(2,1)S(1)} %reshape.96, s32[64]{0:T(128)S(1)} %get-tuple-element.306, ...), kind=kOutput, calls=%fused_computation.2.clone.1 | convolution fusion | flops 144687104 | bytes 4391424 | tf_op jit(solution)/shard_map/while/body/eval_jaxpr/cri,crm->rim/dot_general | solution.py:59
  370.3 5.1 %fusion.117 = (f32[64,128]{1,0:T(8,128)S(1)}, f32[64,128]{1,0:T(8,128)S(1)}, bf16[64,128,128]{1,2,0:T(8,128)(2,1)}) fusion(f32[128,128]{0,1:T(8,128)S(1)} %get-tuple-element.268, bf16[64,64,128]{2,0,1:T(8,128)(2,1)} %get-tuple-element.308, bf16[64,64,128]{2,1,0:T(8,128)(2,1)S(1)} %reshape.96, s32[64]{0:T(128)S(1)} %get-tuple-element.306, ...), kind=kOutput, calls=%fused_computation.2.clone.1 | convolution fusion | flops 144687104 | bytes 4391424 | tf_op jit(solution)/shard_map/while/body/eval_jaxpr/cri,crm->rim/dot_general | solution.py:59
  381.6 5.1 %fusion.117 = (f32[64,128]{1,0:T(8,128)S(1)}, f32[64,128]{1,0:T(8,128)S(1)}, bf16[64,128,128]{1,2,0:T(8,128)(2,1)}) fusion(f32[128,128]{0,1:T(8,128)S(1)} %get-tuple-element.268, bf16[64,64,128]{2,0,1:T(8,128)(2,1)} %get-tuple-element.308, bf16[64,64,128]{2,1,0:T(8,128)(2,1)S(1)} %reshape.96, s32[64]{0:T(128)S(1)} %get-tuple-element.306, ...), kind=kOutput, calls=%fused_computation.2.clone.1 | convolution fusion | flops 144687104 | bytes 4391424 | tf_op jit(solution)/shard_map/while/body/eval_jaxpr/cri,crm->rim/dot_general | solution.py:59
  393.0 5.1 %fusion.117 = (f32[64,128]{1,0:T(8,128)S(1)}, f32[64,128]{1,0:T(8,128)S(1)}, bf16[64,128,128]{1,2,0:T(8,128)(2,1)}) fusion(f32[128,128]{0,1:T(8,128)S(1)} %get-tuple-element.268, bf16[64,64,128]{2,0,1:T(8,128)(2,1)} %get-tuple-element.308, bf16[64,64,128]{2,1,0:T(8,128)(2,1)S(1)} %reshape.96, s32[64]{0:T(128)S(1)} %get-tuple-element.306, ...), kind=kOutput, calls=%fused_computation.2.clone.1 | convolution fusion | flops 144687104 | bytes 4391424 | tf_op jit(solution)/shard_map/while/body/eval_jaxpr/cri,crm->rim/dot_general | solution.py:59
  404.3 5.1 %fusion.117 = (f32[64,128]{1,0:T(8,128)S(1)}, f32[64,128]{1,0:T(8,128)S(1)}, bf16[64,128,128]{1,2,0:T(8,128)(2,1)}) fusion(f32[128,128]{0,1:T(8,128)S(1)} %get-tuple-element.268, bf16[64,64,128]{2,0,1:T(8,128)(2,1)} %get-tuple-element.308, bf16[64,64,128]{2,1,0:T(8,128)(2,1)S(1)} %reshape.96, s32[64]{0:T(128)S(1)} %get-tuple-element.306, ...), kind=kOutput, calls=%fused_computation.2.clone.1 | convolution fusion | flops 144687104 | bytes 4391424 | tf_op jit(solution)/shard_map/while/body/eval_jaxpr/cri,crm->rim/dot_general | solution.py:59
  415.7 5.1 %fusion.117 = (f32[64,128]{1,0:T(8,128)S(1)}, f32[64,128]{1,0:T(8,128)S(1)}, bf16[64,128,128]{1,2,0:T(8,128)(2,1)}) fusion(f32[128,128]{0,1:T(8,128)S(1)} %get-tuple-element.268, bf16[64,64,128]{2,0,1:T(8,128)(2,1)} %get-tuple-element.308, bf16[64,64,128]{2,1,0:T(8,128)(2,1)S(1)} %reshape.96, s32[64]{0:T(128)S(1)} %get-tuple-element.306, ...), kind=kOutput, calls=%fused_computation.2.clone.1 | convolution fusion | flops 144687104 | bytes 4391424 | tf_op jit(solution)/shard_map/while/body/eval_jaxpr/cri,crm->rim/dot_general | solution.py:59
  427.0 5.1 %fusion.117 = (f32[64,128]{1,0:T(8,128)S(1)}, f32[64,128]{1,0:T(8,128)S(1)}, bf16[64,128,128]{1,2,0:T(8,128)(2,1)}) fusion(f32[128,128]{0,1:T(8,128)S(1)} %get-tuple-element.268, bf16[64,64,128]{2,0,1:T(8,128)(2,1)} %get-tuple-element.308, bf16[64,64,128]{2,1,0:T(8,128)(2,1)S(1)} %reshape.96, s32[64]{0:T(128)S(1)} %get-tuple-element.306, ...), kind=kOutput, calls=%fused_computation.2.clone.1 | convolution fusion | flops 144687104 | bytes 4391424 | tf_op jit(solution)/shard_map/while/body/eval_jaxpr/cri,crm->rim/dot_general | solution.py:59
  437.2 5.9 %all-to-all-start.2 = ((f32[8,8,128]{2,0,1:T(8,128)}), f32[8,8,128]{2,0,1:T(8,128)S(1)}, u32[]{:S(2)}, u32[]{:S(2)}) async-start(f32[8,8,128]{2,0,1:T(8,128)} %copy.86), calls=%async_computation.2 | async-start | bytes 65536 | tf_op jit(solution)/shard_map/all_to_all | solution.py:123
  451.1 5.1 %all-to-all-start.1 = ((bf16[8,2,32768]{2,1,0:T(2,128)(2,1)}), bf16[8,2,32768]{2,1,0:T(2,128)(2,1)S(1)}, u32[]{:S(2)}, u32[]{:S(2)}) async-start(bf16[8,2,32768]{2,1,0:T(2,128)(2,1)} %reshape.93), calls=%async_computation.1 | async-start | bytes 2097152 | tf_op jit(solution)/shard_map/all_to_all | solution.py:122
  456.2 26.6 %all-to-all-done.1 = bf16[8,2,32768]{2,1,0:T(2,128)(2,1)S(1)} async-done(((bf16[8,2,32768]{2,1,0:T(2,128)(2,1)}), bf16[8,2,32768]{2,1,0:T(2,128)(2,1)S(1)}, u32[]{:S(2)}, u32[]{:S(2)}) %all-to-all-start.1) | async-done | bytes 1048608 | tf_op jit(solution)/shard_map/all_to_all | solution.py:122
  (263 shorter events, 174.6 us)
Async XLA Ops:
  0.6 9.9 %copy-start.7 = (bf16[2,64,64,128]{3,2,1,0:T(8,128)(2,1)S(1)}, bf16[2,64,64,128]{3,2,1,0:T(8,128)(2,1)}, u32[]{:S(2)}) copy-start(bf16[2,64,64,128]{3,2,1,0:T(8,128)(2,1)} %param.6) | copy-start | bytes 6291460
  0.6 9.9 %copy-start.13 = (bf16[9,64,64]{2,1,0:T(8,128)(2,1)S(1)}, bf16[9,64,64]{2,1,0:T(8,128)(2,1)}, u32[]{:S(2)}) copy-start(bf16[9,64,64]{2,1,0:T(8,128)(2,1)} %param.7) | copy-start | bytes 221188
  3.7 12.0 %copy-start.10 = (bf16[2,64,64,128]{3,1,2,0:T(8,128)(2,1)}, bf16[2,64,64,128]{3,1,2,0:T(8,128)(2,1)S(1)}, u32[]{:S(2)}) copy-start(bf16[2,64,64,128]{3,1,2,0:T(8,128)(2,1)S(1)} %copy.65) | copy-start | bytes 6291460
  3.8 10.4 %collective-permute-start = (bf16[2,64,2,128]{3,1,2,0:T(8,128)(2,1)S(1)}, bf16[2,64,2,128]{3,1,2,0:T(8,128)(2,1)S(1)}, u32[]{:S(2)}, u32[]{:S(2)}) collective-permute-start(bf16[2,64,2,128]{3,1,2,0:T(8,128)(2,1)S(1)} %get-tuple-element.206), channel_id=1, source_target_pairs={{0,8},{8,16},{16,24},{1,9},{9,17},{17,25},{2,10},{10,18},{18,26},{... | collective-permute-start | bytes 196616 | tf_op jit(solution)/shard_map/ppermute | solution.py:19
  7.2 8.5 %collective-permute-start.1 = (bf16[2,64,2,128]{3,1,2,0:T(8,128)(2,1)S(1)}, bf16[2,64,2,128]{3,1,2,0:T(8,128)(2,1)S(1)}, u32[]{:S(2)}, u32[]{:S(2)}) collective-permute-start(bf16[2,64,2,128]{3,1,2,0:T(8,128)(2,1)S(1)} %get-tuple-element.207), channel_id=1, source_target_pairs={{8,0},{16,8},{24,16},{9,1},{17,9},{25,17},{10,2},{18,10},{26,18},{... | collective-permute-start | bytes 196616 | tf_op jit(solution)/shard_map/ppermute | solution.py:22
  22.7 28.0 %collective-permute-start.3 = (bf16[2,64,68,2]{2,1,3,0:T(8,128)(2,1)S(1)}, bf16[2,64,68,2]{2,1,3,0:T(8,128)(2,1)S(1)}, u32[]{:S(2)}, u32[]{:S(2)}) collective-permute-start(bf16[2,64,68,2]{2,1,3,0:T(8,128)(2,1)S(1)} %copy.72), channel_id=1, source_target_pairs={{1,0},{2,1},{3,2},{4,3},{5,4},{6,5},{7,6},{9,8},{10,9},{11,10},{12... | collective-permute-start | bytes 104456 | tf_op jit(solution)/shard_map/ppermute | solution.py:22
  27.7 7.5 %copy-start.11 = (bf16[2,64,64,128]{3,1,2,0:T(8,128)(2,1)S(1)}, bf16[2,64,64,128]{3,1,2,0:T(8,128)(2,1)}, u32[]{:S(2)}) copy-start(bf16[2,64,64,128]{3,1,2,0:T(8,128)(2,1)} %copy-done.10) | copy-start | bytes 6291460
  27.7 10.1 %collective-permute-start.2 = (bf16[2,64,68,2]{2,1,3,0:T(8,128)(2,1)S(1)}, bf16[2,64,68,2]{2,1,3,0:T(8,128)(2,1)S(1)}, u32[]{:S(2)}, u32[]{:S(2)}) collective-permute-start(bf16[2,64,68,2]{2,1,3,0:T(8,128)(2,1)S(1)} %copy.69), channel_id=1, source_target_pairs={{0,1},{1,2},{2,3},{3,4},{4,5},{5,6},{6,7},{8,9},{9,10},{10,11},{11... | collective-permute-start | bytes 104456 | tf_op jit(solution)/shard_map/ppermute | solution.py:19
  42.7 4.9 copy-start.5
  55.2 5.3 %copy-start.4 = (bf16[2,64,68,2]{3,1,2,0:T(8,128)(2,1)S(1)}, bf16[2,64,68,2]{3,1,2,0:T(8,128)(2,1)}, u32[]{:S(2)}) copy-start(bf16[2,64,68,2]{3,1,2,0:T(8,128)(2,1)} %copy.73) | copy-start | bytes 104452
  60.5 3.5 copy-start.6
  67.1 31.5 %copy-start.14 = (bf16[9,64,64]{2,1,0:T(8,128)(2,1)S(1)}, bf16[9,64,64]{2,1,0:T(8,128)(2,1)}, u32[]{:S(2)}) copy-start(bf16[9,64,64]{2,1,0:T(8,128)(2,1)} %param.8) | copy-start | bytes 221188
  79.7 22.0 %copy-start = (bf16[2,64,64,128]{3,1,2,0:T(8,128)(2,1)}, bf16[2,64,64,128]{3,1,2,0:T(8,128)(2,1)S(1)}, u32[]{:S(2)}) copy-start(bf16[2,64,64,128]{3,1,2,0:T(8,128)(2,1)S(1)} %fusion.11) | copy-start | bytes 6291460
  79.7 21.6 %collective-permute-start.4 = (bf16[2,64,4,128]{3,1,2,0:T(8,128)(2,1)S(1)}, bf16[2,64,4,128]{3,1,2,0:T(8,128)(2,1)S(1)}, u32[]{:S(2)}, u32[]{:S(2)}) collective-permute-start(bf16[2,64,4,128]{3,1,2,0:T(8,128)(2,1)S(1)} %get-tuple-element.204), channel_id=1, source_target_pairs={{0,8},{8,16},{16,24},{1,9},{9,17},{17,25},{2,10},{10,18},{18,26},{... | collective-permute-start | bytes 393224 | tf_op jit(solution)/shard_map/ppermute | solution.py:19
  82.2 19.1 %collective-permute-start.5 = (bf16[2,64,4,128]{3,1,2,0:T(8,128)(2,1)S(1)}, bf16[2,64,4,128]{3,1,2,0:T(8,128)(2,1)S(1)}, u32[]{:S(2)}, u32[]{:S(2)}) collective-permute-start(bf16[2,64,4,128]{3,1,2,0:T(8,128)(2,1)S(1)} %get-tuple-element.205), channel_id=1, source_target_pairs={{8,0},{16,8},{24,16},{9,1},{17,9},{25,17},{10,2},{18,10},{26,18},{... | collective-permute-start | bytes 393224 | tf_op jit(solution)/shard_map/ppermute | solution.py:22
  105.0 12.1 %copy-start.1 = (bf16[2,64,64,128]{3,1,2,0:T(8,128)(2,1)S(1)}, bf16[2,64,64,128]{3,1,2,0:T(8,128)(2,1)}, u32[]{:S(2)}) copy-start(bf16[2,64,64,128]{3,1,2,0:T(8,128)(2,1)} %copy-done) | copy-start | bytes 6291460
  109.2 13.3 %collective-permute-start.6 = (bf16[2,64,72,4]{2,1,3,0:T(8,128)(2,1)S(1)}, bf16[2,64,72,4]{2,1,3,0:T(8,128)(2,1)S(1)}, u32[]{:S(2)}, u32[]{:S(2)}) collective-permute-start(bf16[2,64,72,4]{2,1,3,0:T(8,128)(2,1)S(1)} %copy.76), channel_id=1, source_target_pairs={{0,1},{1,2},{2,3},{3,4},{4,5},{5,6},{6,7},{8,9},{9,10},{10,11},{11... | collective-permute-start | bytes 221192 | tf_op jit(solution)/shard_map/ppermute | solution.py:19
  115.8 11.4 %collective-permute-start.7 = (bf16[2,64,72,4]{2,1,3,0:T(8,128)(2,1)S(1)}, bf16[2,64,72,4]{2,1,3,0:T(8,128)(2,1)S(1)}, u32[]{:S(2)}, u32[]{:S(2)}) collective-permute-start(bf16[2,64,72,4]{2,1,3,0:T(8,128)(2,1)S(1)} %copy.78), channel_id=1, source_target_pairs={{1,0},{2,1},{3,2},{4,3},{5,4},{6,5},{7,6},{9,8},{10,9},{11,10},{12... | collective-permute-start | bytes 221192 | tf_op jit(solution)/shard_map/ppermute | solution.py:22
  137.9 8.8 %copy-start.9 = (bf16[2,64,72,132]{3,1,2,0:T(8,128)(2,1)}, bf16[2,64,72,132]{3,1,2,0:T(8,128)(2,1)S(1)}, u32[]{:S(2)}) copy-start(bf16[2,64,72,132]{3,1,2,0:T(8,128)(2,1)S(1)} %get-tuple-element.196) | copy-start | bytes 7299076
  149.5 2.8 copy-start.8
  149.5 4.3 copy-start.12
  171.1 8.2 %copy-start.15 = (s32[2,8,1]{1,2,0:T(1,128)S(1)}, s32[2,8,1]{1,2,0:T(1,128)}, u32[]{:S(2)}) copy-start(s32[2,8,1]{1,2,0:T(1,128)} %param.9) | copy-start | bytes 196
  172.7 55.7 %all-to-all-start = ((bf16[2,64,64,128]{3,1,0,2:T(8,128)(2,1)}), bf16[2,64,64,128]{3,1,0,2:T(8,128)(2,1)S(1)}, u32[]{:S(2)}, u32[]{:S(2)}) async-start(bf16[2,64,64,128]{3,1,0,2:T(8,128)(2,1)} %copy.80), calls=%async_computation | async-start | bytes 4194304 | tf_op jit(solution)/shard_map/all_to_all | solution.py:91
  234.0 5.2 %copy-start.2 = (f32[64,64,128]{2,0,1:T(8,128)S(1)}, f32[64,64,128]{2,0,1:T(8,128)}, u32[]{:S(2)}) copy-start(f32[64,64,128]{2,0,1:T(8,128)} %get-tuple-element.291) | copy-start | bytes 6291460 | tf_op jit(solution)/shard_map/while
  242.2 1.3 copy-start.3
  245.4 5.2 %copy-start.2 = (f32[64,64,128]{2,0,1:T(8,128)S(1)}, f32[64,64,128]{2,0,1:T(8,128)}, u32[]{:S(2)}) copy-start(f32[64,64,128]{2,0,1:T(8,128)} %get-tuple-element.291) | copy-start | bytes 6291460 | tf_op jit(solution)/shard_map/while
  253.6 1.3 copy-start.3
  256.7 5.2 %copy-start.2 = (f32[64,64,128]{2,0,1:T(8,128)S(1)}, f32[64,64,128]{2,0,1:T(8,128)}, u32[]{:S(2)}) copy-start(f32[64,64,128]{2,0,1:T(8,128)} %get-tuple-element.291) | copy-start | bytes 6291460 | tf_op jit(solution)/shard_map/while
  264.9 1.3 copy-start.3
  268.1 5.2 %copy-start.2 = (f32[64,64,128]{2,0,1:T(8,128)S(1)}, f32[64,64,128]{2,0,1:T(8,128)}, u32[]{:S(2)}) copy-start(f32[64,64,128]{2,0,1:T(8,128)} %get-tuple-element.291) | copy-start | bytes 6291460 | tf_op jit(solution)/shard_map/while
  279.4 5.2 %copy-start.2 = (f32[64,64,128]{2,0,1:T(8,128)S(1)}, f32[64,64,128]{2,0,1:T(8,128)}, u32[]{:S(2)}) copy-start(f32[64,64,128]{2,0,1:T(8,128)} %get-tuple-element.291) | copy-start | bytes 6291460 | tf_op jit(solution)/shard_map/while
  290.8 5.2 %copy-start.2 = (f32[64,64,128]{2,0,1:T(8,128)S(1)}, f32[64,64,128]{2,0,1:T(8,128)}, u32[]{:S(2)}) copy-start(f32[64,64,128]{2,0,1:T(8,128)} %get-tuple-element.291) | copy-start | bytes 6291460 | tf_op jit(solution)/shard_map/while
  302.1 5.2 %copy-start.2 = (f32[64,64,128]{2,0,1:T(8,128)S(1)}, f32[64,64,128]{2,0,1:T(8,128)}, u32[]{:S(2)}) copy-start(f32[64,64,128]{2,0,1:T(8,128)} %get-tuple-element.291) | copy-start | bytes 6291460 | tf_op jit(solution)/shard_map/while
  313.5 5.2 %copy-start.2 = (f32[64,64,128]{2,0,1:T(8,128)S(1)}, f32[64,64,128]{2,0,1:T(8,128)}, u32[]{:S(2)}) copy-start(f32[64,64,128]{2,0,1:T(8,128)} %get-tuple-element.291) | copy-start | bytes 6291460 | tf_op jit(solution)/shard_map/while
  324.9 5.2 %copy-start.2 = (f32[64,64,128]{2,0,1:T(8,128)S(1)}, f32[64,64,128]{2,0,1:T(8,128)}, u32[]{:S(2)}) copy-start(f32[64,64,128]{2,0,1:T(8,128)} %get-tuple-element.291) | copy-start | bytes 6291460 | tf_op jit(solution)/shard_map/while
  336.2 5.2 %copy-start.2 = (f32[64,64,128]{2,0,1:T(8,128)S(1)}, f32[64,64,128]{2,0,1:T(8,128)}, u32[]{:S(2)}) copy-start(f32[64,64,128]{2,0,1:T(8,128)} %get-tuple-element.291) | copy-start | bytes 6291460 | tf_op jit(solution)/shard_map/while
  347.6 5.2 %copy-start.2 = (f32[64,64,128]{2,0,1:T(8,128)S(1)}, f32[64,64,128]{2,0,1:T(8,128)}, u32[]{:S(2)}) copy-start(f32[64,64,128]{2,0,1:T(8,128)} %get-tuple-element.291) | copy-start | bytes 6291460 | tf_op jit(solution)/shard_map/while
  358.9 5.2 %copy-start.2 = (f32[64,64,128]{2,0,1:T(8,128)S(1)}, f32[64,64,128]{2,0,1:T(8,128)}, u32[]{:S(2)}) copy-start(f32[64,64,128]{2,0,1:T(8,128)} %get-tuple-element.291) | copy-start | bytes 6291460 | tf_op jit(solution)/shard_map/while
  370.3 5.2 %copy-start.2 = (f32[64,64,128]{2,0,1:T(8,128)S(1)}, f32[64,64,128]{2,0,1:T(8,128)}, u32[]{:S(2)}) copy-start(f32[64,64,128]{2,0,1:T(8,128)} %get-tuple-element.291) | copy-start | bytes 6291460 | tf_op jit(solution)/shard_map/while
  381.6 5.2 %copy-start.2 = (f32[64,64,128]{2,0,1:T(8,128)S(1)}, f32[64,64,128]{2,0,1:T(8,128)}, u32[]{:S(2)}) copy-start(f32[64,64,128]{2,0,1:T(8,128)} %get-tuple-element.291) | copy-start | bytes 6291460 | tf_op jit(solution)/shard_map/while
  393.0 5.2 %copy-start.2 = (f32[64,64,128]{2,0,1:T(8,128)S(1)}, f32[64,64,128]{2,0,1:T(8,128)}, u32[]{:S(2)}) copy-start(f32[64,64,128]{2,0,1:T(8,128)} %get-tuple-element.291) | copy-start | bytes 6291460 | tf_op jit(solution)/shard_map/while
  404.3 5.2 %copy-start.2 = (f32[64,64,128]{2,0,1:T(8,128)S(1)}, f32[64,64,128]{2,0,1:T(8,128)}, u32[]{:S(2)}) copy-start(f32[64,64,128]{2,0,1:T(8,128)} %get-tuple-element.291) | copy-start | bytes 6291460 | tf_op jit(solution)/shard_map/while
  412.5 1.3 copy-start.3
  415.7 5.2 %copy-start.2 = (f32[64,64,128]{2,0,1:T(8,128)S(1)}, f32[64,64,128]{2,0,1:T(8,128)}, u32[]{:S(2)}) copy-start(f32[64,64,128]{2,0,1:T(8,128)} %get-tuple-element.291) | copy-start | bytes 6291460 | tf_op jit(solution)/shard_map/while
  423.8 1.3 copy-start.3
  427.0 5.2 %copy-start.2 = (f32[64,64,128]{2,0,1:T(8,128)S(1)}, f32[64,64,128]{2,0,1:T(8,128)}, u32[]{:S(2)}) copy-start(f32[64,64,128]{2,0,1:T(8,128)} %get-tuple-element.291) | copy-start | bytes 6291460 | tf_op jit(solution)/shard_map/while
  437.2 13.9 %all-to-all-start.2 = ((f32[8,8,128]{2,0,1:T(8,128)}), f32[8,8,128]{2,0,1:T(8,128)S(1)}, u32[]{:S(2)}, u32[]{:S(2)}) async-start(f32[8,8,128]{2,0,1:T(8,128)} %copy.86), calls=%async_computation.2 | async-start | bytes 65536 | tf_op jit(solution)/shard_map/all_to_all | solution.py:123
  451.1 31.7 %all-to-all-start.1 = ((bf16[8,2,32768]{2,1,0:T(2,128)(2,1)}), bf16[8,2,32768]{2,1,0:T(2,128)(2,1)S(1)}, u32[]{:S(2)}, u32[]{:S(2)}) async-start(bf16[8,2,32768]{2,1,0:T(2,128)(2,1)} %reshape.93), calls=%async_computation.1 | async-start | bytes 2097152 | tf_op jit(solution)/shard_map/all_to_all | solution.py:122
  (13 other events, 17.4 us)
where the time goes:
time: 497 us; the launch traced here: 488 us
  matrix products  227 us (46%)
  local copies, waits for them, and re-layouts  120 us (24%)
  starting transfers between devices  51.6 us (10%)
  blocking collectives  41.5 us (8%)
  waiting for transfers between devices  33.9 us (7%)
  other arithmetic  11 us (2%)
    dot_general x18, matrix products, hop_terms(): jnp.einsum('cri,crm->rim', source_descriptors, key_feats, preferred_eleme...  92.6 us
    dot_general x18, matrix products, convolution_layer(): jnp.einsum('oc,nchw->nohw', weights[3 * row_tap + horizontal_offset], win...  80.5 us
    dot_general x18, matrix products, hop_terms(): jnp.einsum('rim,crm->cri', rounded, key_feats, preferred_element_type=jnp...  54.3 us
    all_gather x1, blocking collectives, per_device(): gathered = lax.all_gather(search_ranges, 'cols', axis=2, tiled=True)  41.5 us
    all_to_all x1, waiting for transfers between devices, per_device(): lax.all_to_all(matched_rows, 'cols', split_axis=2, concat_axis=1, tiled=T...  26.6 us
    while x72, local copies, waits for them, and re-layouts  23.5 us
    dynamic_slice x18, local copies, waits for them, and re-layouts, accumulate(): lax.dynamic_slice_in_dim(padded, (HOPS - 1 - hop_index) * segment, full_w...  23.3 us
    ppermute x4, starting transfers between devices, with_halo(): lax.ppermute(lax.slice_in_dim(block, 0, width, axis=dim), axis, backward)  22.3 us
  transfers between devices with their start and end apart: 11, of which 2 were waited for; matrix products, arithmetic and copies ran while one was open for 11% of the time, Pallas kernels for 0%

commit v1 on v0

--- a/solution.py
+++ b/solution.py
@@ -89,7 +89,14 @@
     band_rows = count_rows // peer_count
     full_width = segment * peer_count
     whole_rows = lax.all_to_all(unit_feats, "cols", split_axis=2, concat_axis=3, tiled=True)
-    gathered = lax.all_gather(search_ranges, "cols", axis=2, tiled=True)
+    count_2 = lax.axis_size("cols")
+    right = [(i_2, (i_2 + 1) % count_2) for i_2 in range(count_2)]
+    parts = [search_ranges]
+    for far in range(1, count_2):
+        parts = [lax.ppermute(parts[0], "cols", right), *parts]
+    full = jnp.concatenate(parts, axis=2)
+    turn = (lax.axis_index("cols") + 1) * parts[-1].shape[2]
+    gathered = jnp.roll(full, turn, axis=2)
     spread_rows = jnp.repeat(gathered, RG, axis=1)
     own_ranges = lax.dynamic_slice_in_dim(spread_rows, column * band_rows, band_rows, 1).reshape(
         2, band_rows * peer_count

time: 497 us -> 513 us (1.032)
  waiting for transfers between devices: 33.9 us -> 91.7 us
  blocking collectives: 41.5 us -> 0 us
    ppermute x0 -> x7, waiting for transfers between devices: none -> 65.1 us  [per_device(): parts = [lax.ppermute(parts[0], 'cols', right), *parts]]
    all_gather x1 -> x0, blocking collectives: 41.5 us -> none  [per_device(): gathered = lax.all_gather(search_ranges, 'cols', axis=2, tiled=True)]
    all_to_all x1, waiting for transfers between devices: 7.28 us -> 0.01 us  [per_device(): lax.all_to_all(unit_feats, 'cols', split_axis=2, concat_axis=3, tiled=True)]
  transfers between devices with their start and end apart: 11 -> 18, of which waited for: 2 -> 8; matrix products, arithmetic and copies ran while one was open for 11% -> 11% of each run, Pallas kernels for 0% -> 0%
where the time goes in v1:
time: 513 us; the launch traced here: 504 us
  matrix products  227 us (44%)
  local copies, waits for them, and re-layouts  120 us (23%)
  waiting for transfers between devices  91.7 us (18%)
  starting transfers between devices  51.5 us (10%)
  other arithmetic  11 us (2%)
    dot_general x18, matrix products, hop_terms(): jnp.einsum('cri,crm->rim', source_descriptors, key_feats, preferred_eleme...  92.3 us
    dot_general x18, matrix products, convolution_layer(): jnp.einsum('oc,nchw->nohw', weights[3 * row_tap + horizontal_offset], win...  80.7 us
    ppermute x7, waiting for transfers between devices, per_device(): parts = [lax.ppermute(parts[0], 'cols', right), *parts]  65.1 us
    dot_general x18, matrix products, hop_terms(): jnp.einsum('rim,crm->cri', rounded, key_feats, preferred_element_type=jnp...  54.2 us
    all_to_all x1, waiting for transfers between devices, per_device(): lax.all_to_all(matched_rows, 'cols', split_axis=2, concat_axis=1, tiled=T...  26.6 us
    while x72, local copies, waits for them, and re-layouts  23.5 us
    dynamic_slice x18, local copies, waits for them, and re-layouts, accumulate(): lax.dynamic_slice_in_dim(padded, (HOPS - 1 - hop_index) * segment, full_w...  23.3 us
    ppermute x4, starting transfers between devices, with_halo(): lax.ppermute(lax.slice_in_dim(block, 0, width, axis=dim), axis, backward)  22.8 us
  transfers between devices with their start and end apart: 18, of which 8 were waited for; matrix products, arithmetic and copies ran while one was open for 11% of the time, Pallas kernels for 0%

profile of v1, /device:TPU:4, one launch (start us, length us, event | category | flops | bytes accessed | tf_op | source)
XLA Modules:
  0.0 504.3 jit_solution(3718636443606451689)
XLA Ops:
  3.8 3.4 collective-permute-start.7
  7.2 3.3 collective-permute-start.8
  10.6 3.7 fusion.64
  19.0 3.7 copy.70
  24.0 3.7 copy.67
  30.9 4.3 fusion.44
  37.9 4.8 copy.68
  42.7 4.9 fusion.19
  50.7 4.5 copy.71
  55.2 5.3 %fusion.16 = f32[2,64,128,64]{2,3,1,0:T(8,128)} fusion(bf16[2,64,68,128]{3,1,2,0:T(8,128)(2,1)S(1)} %constant_dynamic-update-slice_fusion, bf16[2,64,68,2]{3,1,2,0:T(8,128)(2,1)} %copy.71, bf16[9,64,64]{2,1,0:T(8,128)(2,1)S(1)} %copy-done.13), kind=kOutput, calls=%fused_computation.40 | convolution fusion | flops 138412032 | bytes 6473728 | tf_op jit(solution)/shard_map/oc,nchw->nohw/dot_general | solution.py:40
  60.5 3.5 fusion.13
  67.2 12.5 %fusion.11 = bf16[2,64,64,128]{3,1,2,0:T(8,128)(2,1)S(1)} fusion(f32[2,64,128,64]{2,3,1,0:T(8,128)} %fusion.44, f32[2,64,128,64]{2,3,1,0:T(8,128)} %fusion.46, f32[2,64,128,64]{2,3,1,0:T(8,128)} %fusion.13, f32[2,64,128,64]{2,3,1,0:T(8,128)} %fusion.64, f32[2,64,128,64]{2,3,1,0:T(8,128)} %fusion.19, f32[2,64,128,64]{2,3,1,0:T(8,128)} %fusion.16, ...), kind=kOutput, calls=%fused_computation.35 | convolution fusion | flops 152043520 | bytes 40124416 | tf_op jit(solution)/shard_map/oc,nchw->nohw/dot_general | solution.py:40
  82.3 16.8 %collective-permute-start.12 = (bf16[2,64,4,128]{3,1,2,0:T(8,128)(2,1)S(1)}, bf16[2,64,4,128]{3,1,2,0:T(8,128)(2,1)S(1)}, u32[]{:S(2)}, u32[]{:S(2)}) collective-permute-start(bf16[2,64,4,128]{3,1,2,0:T(8,128)(2,1)S(1)} %get-tuple-element.205), channel_id=1, source_target_pairs={{8,0},{16,8},{24,16},{9,1},{17,9},{25,17},{10,2},{18,10},{26,18},{... | collective-permute-start | bytes 393224 | tf_op jit(solution)/shard_map/ppermute | solution.py:22
  105.5 4.2 copy.74
  112.2 4.0 copy.76
  123.0 4.7 copy.75
  127.7 4.8 copy.77
  132.5 5.9 %pad_maximum_fusion = (bf16[2,64,72,132]{3,1,2,0:T(8,128)(2,1)S(1)}, bf16[2,64,72,132]{3,1,2,0:T(8,128)(2,1)S(1)}) fusion(bf16[2,64,72,4]{3,1,2,0:T(8,128)(2,1)} %copy.77, bf16[2,64,4,128]{3,1,2,0:T(8,128)(2,1)S(1)} %collective-permute-done.12, bf16[2,64,64,128]{3,1,2,0:T(8,128)(2,1)S(1)} %copy-done.1, ...), kind=kLoop, calls=%fused_computation.25 | loop fusion | flops 19464192 | bytes 7372800 | tf_op jit(solution)/shard_map/concatenate | solution.py:23
  154.4 15.0 %fusion.5 = (f32[2,64,128]{2,1,0:T(8,128)S(1)}, bf16[2,64,64,128]{3,1,2,0:T(8,128)(2,1)}) fusion(bf16[2,64,72,132]{3,1,2,0:T(8,128)(2,1)} %copy-done.9, bf16[9,64,64]{2,1,0:T(8,128)(2,1)S(1)} %copy-done.14, f32[2,64,128,64]{2,3,1,0:T(8,128)} %fusion.28, f32[2,64,128,64]{2,3,1,0:T(8,128)} %fusion.30, f32[2,64,128,64]{2,3,1,0:T(8,128)} %fusion.32, ...), kind=kOutput, calls=%fused_computation.26 | convolution fusion | flops 148881408 | bytes 39927808 | tf_op jit(solution)/shard_map/oc,nchw->nohw/dot_general | solution.py:40
  173.3 6.6 %all-to-all-start = ((bf16[2,64,64,128]{3,1,0,2:T(8,128)(2,1)}), bf16[2,64,64,128]{3,1,0,2:T(8,128)(2,1)S(1)}, u32[]{:S(2)}, u32[]{:S(2)}) async-start(bf16[2,64,64,128]{3,1,0,2:T(8,128)(2,1)} %copy.78), calls=%async_computation | async-start | bytes 4194304 | tf_op jit(solution)/shard_map/all_to_all | solution.py:91
  180.4 37.8 %collective-permute-done = s32[2,8,1]{1,2,0:T(1,128)S(1)} collective-permute-done((s32[2,8,1]{1,2,0:T(1,128)S(1)}, s32[2,8,1]{1,2,0:T(1,128)S(1)}, u32[]{:S(2)}, u32[]{:S(2)}) %collective-permute-start) | collective-permute-done | bytes 96 | tf_op jit(solution)/shard_map/ppermute | solution.py:96
  218.2 4.8 collective-permute-done.1
  223.0 4.8 collective-permute-done.2
  229.2 3.4 collective-permute-done.3
  232.6 4.8 collective-permute-done.4
  237.4 4.8 collective-permute-done.5
  242.4 4.8 collective-permute-done.6
  251.3 204.0 %while.18 = (s32[]{:T(128)}, f32[64,128]{1,0:T(8,128)S(1)}, f32[64,128]{1,0:T(8,128)S(1)}, f32[64,64,128]{2,0,1:T(8,128)}, s32[64]{0:T(128)S(1)}, /*index=5*/s32...) while((s32[]{:T(128)}, f32[64,128]{1,0:T(8,128)S(1)}, ...), condition=%wide.region_4.5_spmd.clone, body=%wide.region_1.4_spmd.clone.sunk | while | flops 280019072 | bytes 33031948 | solution.py:120
  253.1 5.1 %fusion.117 = (f32[64,128]{1,0:T(8,128)S(1)}, f32[64,128]{1,0:T(8,128)S(1)}, bf16[64,128,128]{1,2,0:T(8,128)(2,1)}) fusion(f32[128,128]{0,1:T(8,128)S(1)} %get-tuple-element.268, bf16[64,64,128]{2,0,1:T(8,128)(2,1)} %get-tuple-element.308, bf16[64,64,128]{2,1,0:T(8,128)(2,1)S(1)} %reshape.96, s32[64]{0:T(128)S(1)} %get-tuple-element.306, ...), kind=kOutput, calls=%fused_computation.2.clone.1 | convolution fusion | flops 144687104 | bytes 4391424 | tf_op jit(solution)/shard_map/while/body/eval_jaxpr/cri,crm->rim/dot_general | solution.py:59
  264.5 5.1 %fusion.117 = (f32[64,128]{1,0:T(8,128)S(1)}, f32[64,128]{1,0:T(8,128)S(1)}, bf16[64,128,128]{1,2,0:T(8,128)(2,1)}) fusion(f32[128,128]{0,1:T(8,128)S(1)} %get-tuple-element.268, bf16[64,64,128]{2,0,1:T(8,128)(2,1)} %get-tuple-element.308, bf16[64,64,128]{2,1,0:T(8,128)(2,1)S(1)} %reshape.96, s32[64]{0:T(128)S(1)} %get-tuple-element.306, ...), kind=kOutput, calls=%fused_computation.2.clone.1 | convolution fusion | flops 144687104 | bytes 4391424 | tf_op jit(solution)/shard_map/while/body/eval_jaxpr/cri,crm->rim/dot_general | solution.py:59
  275.8 5.1 %fusion.117 = (f32[64,128]{1,0:T(8,128)S(1)}, f32[64,128]{1,0:T(8,128)S(1)}, bf16[64,128,128]{1,2,0:T(8,128)(2,1)}) fusion(f32[128,128]{0,1:T(8,128)S(1)} %get-tuple-element.268, bf16[64,64,128]{2,0,1:T(8,128)(2,1)} %get-tuple-element.308, bf16[64,64,128]{2,1,0:T(8,128)(2,1)S(1)} %reshape.96, s32[64]{0:T(128)S(1)} %get-tuple-element.306, ...), kind=kOutput, calls=%fused_computation.2.clone.1 | convolution fusion | flops 144687104 | bytes 4391424 | tf_op jit(solution)/shard_map/while/body/eval_jaxpr/cri,crm->rim/dot_general | solution.py:59
  287.1 5.1 %fusion.117 = (f32[64,128]{1,0:T(8,128)S(1)}, f32[64,128]{1,0:T(8,128)S(1)}, bf16[64,128,128]{1,2,0:T(8,128)(2,1)}) fusion(f32[128,128]{0,1:T(8,128)S(1)} %get-tuple-element.268, bf16[64,64,128]{2,0,1:T(8,128)(2,1)} %get-tuple-element.308, bf16[64,64,128]{2,1,0:T(8,128)(2,1)S(1)} %reshape.96, s32[64]{0:T(128)S(1)} %get-tuple-element.306, ...), kind=kOutput, calls=%fused_computation.2.clone.1 | convolution fusion | flops 144687104 | bytes 4391424 | tf_op jit(solution)/shard_map/while/body/eval_jaxpr/cri,crm->rim/dot_general | solution.py:59
  298.5 5.1 %fusion.117 = (f32[64,128]{1,0:T(8,128)S(1)}, f32[64,128]{1,0:T(8,128)S(1)}, bf16[64,128,128]{1,2,0:T(8,128)(2,1)}) fusion(f32[128,128]{0,1:T(8,128)S(1)} %get-tuple-element.268, bf16[64,64,128]{2,0,1:T(8,128)(2,1)} %get-tuple-element.308, bf16[64,64,128]{2,1,0:T(8,128)(2,1)S(1)} %reshape.96, s32[64]{0:T(128)S(1)} %get-tuple-element.306, ...), kind=kOutput, calls=%fused_computation.2.clone.1 | convolution fusion | flops 144687104 | bytes 4391424 | tf_op jit(solution)/shard_map/while/body/eval_jaxpr/cri,crm->rim/dot_general | solution.py:59
  309.8 5.1 %fusion.117 = (f32[64,128]{1,0:T(8,128)S(1)}, f32[64,128]{1,0:T(8,128)S(1)}, bf16[64,128,128]{1,2,0:T(8,128)(2,1)}) fusion(f32[128,128]{0,1:T(8,128)S(1)} %get-tuple-element.268, bf16[64,64,128]{2,0,1:T(8,128)(2,1)} %get-tuple-element.308, bf16[64,64,128]{2,1,0:T(8,128)(2,1)S(1)} %reshape.96, s32[64]{0:T(128)S(1)} %get-tuple-element.306, ...), kind=kOutput, calls=%fused_computation.2.clone.1 | convolution fusion | flops 144687104 | bytes 4391424 | tf_op jit(solution)/shard_map/while/body/eval_jaxpr/cri,crm->rim/dot_general | solution.py:59
  321.1 5.1 %fusion.117 = (f32[64,128]{1,0:T(8,128)S(1)}, f32[64,128]{1,0:T(8,128)S(1)}, bf16[64,128,128]{1,2,0:T(8,128)(2,1)}) fusion(f32[128,128]{0,1:T(8,128)S(1)} %get-tuple-element.268, bf16[64,64,128]{2,0,1:T(8,128)(2,1)} %get-tuple-element.308, bf16[64,64,128]{2,1,0:T(8,128)(2,1)S(1)} %reshape.96, s32[64]{0:T(128)S(1)} %get-tuple-element.306, ...), kind=kOutput, calls=%fused_computation.2.clone.1 | convolution fusion | flops 144687104 | bytes 4391424 | tf_op jit(solution)/shard_map/while/body/eval_jaxpr/cri,crm->rim/dot_general | solution.py:59
  332.5 5.1 %fusion.117 = (f32[64,128]{1,0:T(8,128)S(1)}, f32[64,128]{1,0:T(8,128)S(1)}, bf16[64,128,128]{1,2,0:T(8,128)(2,1)}) fusion(f32[128,128]{0,1:T(8,128)S(1)} %get-tuple-element.268, bf16[64,64,128]{2,0,1:T(8,128)(2,1)} %get-tuple-element.308, bf16[64,64,128]{2,1,0:T(8,128)(2,1)S(1)} %reshape.96, s32[64]{0:T(128)S(1)} %get-tuple-element.306, ...), kind=kOutput, calls=%fused_computation.2.clone.1 | convolution fusion | flops 144687104 | bytes 4391424 | tf_op jit(solution)/shard_map/while/body/eval_jaxpr/cri,crm->rim/dot_general | solution.py:59
  343.8 5.1 %fusion.117 = (f32[64,128]{1,0:T(8,128)S(1)}, f32[64,128]{1,0:T(8,128)S(1)}, bf16[64,128,128]{1,2,0:T(8,128)(2,1)}) fusion(f32[128,128]{0,1:T(8,128)S(1)} %get-tuple-element.268, bf16[64,64,128]{2,0,1:T(8,128)(2,1)} %get-tuple-element.308, bf16[64,64,128]{2,1,0:T(8,128)(2,1)S(1)} %reshape.96, s32[64]{0:T(128)S(1)} %get-tuple-element.306, ...), kind=kOutput, calls=%fused_computation.2.clone.1 | convolution fusion | flops 144687104 | bytes 4391424 | tf_op jit(solution)/shard_map/while/body/eval_jaxpr/cri,crm->rim/dot_general | solution.py:59
  355.1 5.1 %fusion.117 = (f32[64,128]{1,0:T(8,128)S(1)}, f32[64,128]{1,0:T(8,128)S(1)}, bf16[64,128,128]{1,2,0:T(8,128)(2,1)}) fusion(f32[128,128]{0,1:T(8,128)S(1)} %get-tuple-element.268, bf16[64,64,128]{2,0,1:T(8,128)(2,1)} %get-tuple-element.308, bf16[64,64,128]{2,1,0:T(8,128)(2,1)S(1)} %reshape.96, s32[64]{0:T(128)S(1)} %get-tuple-element.306, ...), kind=kOutput, calls=%fused_computation.2.clone.1 | convolution fusion | flops 144687104 | bytes 4391424 | tf_op jit(solution)/shard_map/while/body/eval_jaxpr/cri,crm->rim/dot_general | solution.py:59
  366.5 5.1 %fusion.117 = (f32[64,128]{1,0:T(8,128)S(1)}, f32[64,128]{1,0:T(8,128)S(1)}, bf16[64,128,128]{1,2,0:T(8,128)(2,1)}) fusion(f32[128,128]{0,1:T(8,128)S(1)} %get-tuple-element.268, bf16[64,64,128]{2,0,1:T(8,128)(2,1)} %get-tuple-element.308, bf16[64,64,128]{2,1,0:T(8,128)(2,1)S(1)} %reshape.96, s32[64]{0:T(128)S(1)} %get-tuple-element.306, ...), kind=kOutput, calls=%fused_computation.2.clone.1 | convolution fusion | flops 144687104 | bytes 4391424 | tf_op jit(solution)/shard_map/while/body/eval_jaxpr/cri,crm->rim/dot_general | solution.py:59
  377.8 5.1 %fusion.117 = (f32[64,128]{1,0:T(8,128)S(1)}, f32[64,128]{1,0:T(8,128)S(1)}, bf16[64,128,128]{1,2,0:T(8,128)(2,1)}) fusion(f32[128,128]{0,1:T(8,128)S(1)} %get-tuple-element.268, bf16[64,64,128]{2,0,1:T(8,128)(2,1)} %get-tuple-element.308, bf16[64,64,128]{2,1,0:T(8,128)(2,1)S(1)} %reshape.96, s32[64]{0:T(128)S(1)} %get-tuple-element.306, ...), kind=kOutput, calls=%fused_computation.2.clone.1 | convolution fusion | flops 144687104 | bytes 4391424 | tf_op jit(solution)/shard_map/while/body/eval_jaxpr/cri,crm->rim/dot_general | solution.py:59
  389.2 5.1 %fusion.117 = (f32[64,128]{1,0:T(8,128)S(1)}, f32[64,128]{1,0:T(8,128)S(1)}, bf16[64,128,128]{1,2,0:T(8,128)(2,1)}) fusion(f32[128,128]{0,1:T(8,128)S(1)} %get-tuple-element.268, bf16[64,64,128]{2,0,1:T(8,128)(2,1)} %get-tuple-element.308, bf16[64,64,128]{2,1,0:T(8,128)(2,1)S(1)} %reshape.96, s32[64]{0:T(128)S(1)} %get-tuple-element.306, ...), kind=kOutput, calls=%fused_computation.2.clone.1 | convolution fusion | flops 144687104 | bytes 4391424 | tf_op jit(solution)/shard_map/while/body/eval_jaxpr/cri,crm->rim/dot_general | solution.py:59
  400.5 5.1 %fusion.117 = (f32[64,128]{1,0:T(8,128)S(1)}, f32[64,128]{1,0:T(8,128)S(1)}, bf16[64,128,128]{1,2,0:T(8,128)(2,1)}) fusion(f32[128,128]{0,1:T(8,128)S(1)} %get-tuple-element.268, bf16[64,64,128]{2,0,1:T(8,128)(2,1)} %get-tuple-element.308, bf16[64,64,128]{2,1,0:T(8,128)(2,1)S(1)} %reshape.96, s32[64]{0:T(128)S(1)} %get-tuple-element.306, ...), kind=kOutput, calls=%fused_computation.2.clone.1 | convolution fusion | flops 144687104 | bytes 4391424 | tf_op jit(solution)/shard_map/while/body/eval_jaxpr/cri,crm->rim/dot_general | solution.py:59
  411.8 5.1 %fusion.117 = (f32[64,128]{1,0:T(8,128)S(1)}, f32[64,128]{1,0:T(8,128)S(1)}, bf16[64,128,128]{1,2,0:T(8,128)(2,1)}) fusion(f32[128,128]{0,1:T(8,128)S(1)} %get-tuple-element.268, bf16[64,64,128]{2,0,1:T(8,128)(2,1)} %get-tuple-element.308, bf16[64,64,128]{2,1,0:T(8,128)(2,1)S(1)} %reshape.96, s32[64]{0:T(128)S(1)} %get-tuple-element.306, ...), kind=kOutput, calls=%fused_computation.2.clone.1 | convolution fusion | flops 144687104 | bytes 4391424 | tf_op jit(solution)/shard_map/while/body/eval_jaxpr/cri,crm->rim/dot_general | solution.py:59
  423.2 5.1 %fusion.117 = (f32[64,128]{1,0:T(8,128)S(1)}, f32[64,128]{1,0:T(8,128)S(1)}, bf16[64,128,128]{1,2,0:T(8,128)(2,1)}) fusion(f32[128,128]{0,1:T(8,128)S(1)} %get-tuple-element.268, bf16[64,64,128]{2,0,1:T(8,128)(2,1)} %get-tuple-element.308, bf16[64,64,128]{2,1,0:T(8,128)(2,1)S(1)} %reshape.96, s32[64]{0:T(128)S(1)} %get-tuple-element.306, ...), kind=kOutput, calls=%fused_computation.2.clone.1 | convolution fusion | flops 144687104 | bytes 4391424 | tf_op jit(solution)/shard_map/while/body/eval_jaxpr/cri,crm->rim/dot_general | solution.py:59
  434.5 5.1 %fusion.117 = (f32[64,128]{1,0:T(8,128)S(1)}, f32[64,128]{1,0:T(8,128)S(1)}, bf16[64,128,128]{1,2,0:T(8,128)(2,1)}) fusion(f32[128,128]{0,1:T(8,128)S(1)} %get-tuple-element.268, bf16[64,64,128]{2,0,1:T(8,128)(2,1)} %get-tuple-element.308, bf16[64,64,128]{2,1,0:T(8,128)(2,1)S(1)} %reshape.96, s32[64]{0:T(128)S(1)} %get-tuple-element.306, ...), kind=kOutput, calls=%fused_computation.2.clone.1 | convolution fusion | flops 144687104 | bytes 4391424 | tf_op jit(solution)/shard_map/while/body/eval_jaxpr/cri,crm->rim/dot_general | solution.py:59
  445.8 5.1 %fusion.117 = (f32[64,128]{1,0:T(8,128)S(1)}, f32[64,128]{1,0:T(8,128)S(1)}, bf16[64,128,128]{1,2,0:T(8,128)(2,1)}) fusion(f32[128,128]{0,1:T(8,128)S(1)} %get-tuple-element.268, bf16[64,64,128]{2,0,1:T(8,128)(2,1)} %get-tuple-element.308, bf16[64,64,128]{2,1,0:T(8,128)(2,1)S(1)} %reshape.96, s32[64]{0:T(128)S(1)} %get-tuple-element.306, ...), kind=kOutput, calls=%fused_computation.2.clone.1 | convolution fusion | flops 144687104 | bytes 4391424 | tf_op jit(solution)/shard_map/while/body/eval_jaxpr/cri,crm->rim/dot_general | solution.py:59
  467.3 5.0 all-to-all-start.1
  472.3 26.6 %all-to-all-done.1 = bf16[8,2,32768]{2,1,0:T(2,128)(2,1)S(1)} async-done(((bf16[8,2,32768]{2,1,0:T(2,128)(2,1)}), bf16[8,2,32768]{2,1,0:T(2,128)(2,1)S(1)}, u32[]{:S(2)}, u32[]{:S(2)}) %all-to-all-start.1) | async-done | bytes 1048608 | tf_op jit(solution)/shard_map/all_to_all | solution.py:129
  (278 shorter events, 193.1 us)
Async XLA Ops:
  0.6 9.9 %copy-start.7 = (bf16[2,64,64,128]{3,2,1,0:T(8,128)(2,1)S(1)}, bf16[2,64,64,128]{3,2,1,0:T(8,128)(2,1)}, u32[]{:S(2)}) copy-start(bf16[2,64,64,128]{3,2,1,0:T(8,128)(2,1)} %param.6) | copy-start | bytes 6291460
  0.6 9.9 %copy-start.13 = (bf16[9,64,64]{2,1,0:T(8,128)(2,1)S(1)}, bf16[9,64,64]{2,1,0:T(8,128)(2,1)}, u32[]{:S(2)}) copy-start(bf16[9,64,64]{2,1,0:T(8,128)(2,1)} %param.7) | copy-start | bytes 221188
  3.7 12.0 %copy-start.10 = (bf16[2,64,64,128]{3,1,2,0:T(8,128)(2,1)}, bf16[2,64,64,128]{3,1,2,0:T(8,128)(2,1)S(1)}, u32[]{:S(2)}) copy-start(bf16[2,64,64,128]{3,1,2,0:T(8,128)(2,1)S(1)} %copy.63) | copy-start | bytes 6291460
  3.8 10.5 %collective-permute-start.7 = (bf16[2,64,2,128]{3,1,2,0:T(8,128)(2,1)S(1)}, bf16[2,64,2,128]{3,1,2,0:T(8,128)(2,1)S(1)}, u32[]{:S(2)}, u32[]{:S(2)}) collective-permute-start(bf16[2,64,2,128]{3,1,2,0:T(8,128)(2,1)S(1)} %get-tuple-element.206), channel_id=1, source_target_pairs={{0,8},{8,16},{16,24},{1,9},{9,17},{17,25},{2,10},{10,18},{18,26},{... | collective-permute-start | bytes 196616 | tf_op jit(solution)/shard_map/ppermute | solution.py:19
  7.2 8.6 %collective-permute-start.8 = (bf16[2,64,2,128]{3,1,2,0:T(8,128)(2,1)S(1)}, bf16[2,64,2,128]{3,1,2,0:T(8,128)(2,1)S(1)}, u32[]{:S(2)}, u32[]{:S(2)}) collective-permute-start(bf16[2,64,2,128]{3,1,2,0:T(8,128)(2,1)S(1)} %get-tuple-element.207), channel_id=1, source_target_pairs={{8,0},{16,8},{24,16},{9,1},{17,9},{25,17},{10,2},{18,10},{26,18},{... | collective-permute-start | bytes 196616 | tf_op jit(solution)/shard_map/ppermute | solution.py:22
  22.7 28.0 %collective-permute-start.10 = (bf16[2,64,68,2]{2,1,3,0:T(8,128)(2,1)S(1)}, bf16[2,64,68,2]{2,1,3,0:T(8,128)(2,1)S(1)}, u32[]{:S(2)}, u32[]{:S(2)}) collective-permute-start(bf16[2,64,68,2]{2,1,3,0:T(8,128)(2,1)S(1)} %copy.70), channel_id=1, source_target_pairs={{1,0},{2,1},{3,2},{4,3},{5,4},{6,5},{7,6},{9,8},{10,9},{11,10},{12... | collective-permute-start | bytes 104456 | tf_op jit(solution)/shard_map/ppermute | solution.py:22
  27.7 7.5 %copy-start.11 = (bf16[2,64,64,128]{3,1,2,0:T(8,128)(2,1)S(1)}, bf16[2,64,64,128]{3,1,2,0:T(8,128)(2,1)}, u32[]{:S(2)}) copy-start(bf16[2,64,64,128]{3,1,2,0:T(8,128)(2,1)} %copy-done.10) | copy-start | bytes 6291460
  27.7 10.2 %collective-permute-start.9 = (bf16[2,64,68,2]{2,1,3,0:T(8,128)(2,1)S(1)}, bf16[2,64,68,2]{2,1,3,0:T(8,128)(2,1)S(1)}, u32[]{:S(2)}, u32[]{:S(2)}) collective-permute-start(bf16[2,64,68,2]{2,1,3,0:T(8,128)(2,1)S(1)} %copy.67), channel_id=1, source_target_pairs={{0,1},{1,2},{2,3},{3,4},{4,5},{5,6},{6,7},{8,9},{9,10},{10,11},{11... | collective-permute-start | bytes 104456 | tf_op jit(solution)/shard_map/ppermute | solution.py:19
  42.7 4.9 copy-start.5
  55.2 5.3 %copy-start.4 = (bf16[2,64,68,2]{3,1,2,0:T(8,128)(2,1)S(1)}, bf16[2,64,68,2]{3,1,2,0:T(8,128)(2,1)}, u32[]{:S(2)}) copy-start(bf16[2,64,68,2]{3,1,2,0:T(8,128)(2,1)} %copy.71) | copy-start | bytes 104452
  67.2 31.9 %copy-start.14 = (bf16[9,64,64]{2,1,0:T(8,128)(2,1)S(1)}, bf16[9,64,64]{2,1,0:T(8,128)(2,1)}, u32[]{:S(2)}) copy-start(bf16[9,64,64]{2,1,0:T(8,128)(2,1)} %param.8) | copy-start | bytes 221188
  79.7 22.4 %copy-start = (bf16[2,64,64,128]{3,1,2,0:T(8,128)(2,1)}, bf16[2,64,64,128]{3,1,2,0:T(8,128)(2,1)S(1)}, u32[]{:S(2)}) copy-start(bf16[2,64,64,128]{3,1,2,0:T(8,128)(2,1)S(1)} %fusion.11) | copy-start | bytes 6291460
  79.8 22.1 %collective-permute-start.11 = (bf16[2,64,4,128]{3,1,2,0:T(8,128)(2,1)S(1)}, bf16[2,64,4,128]{3,1,2,0:T(8,128)(2,1)S(1)}, u32[]{:S(2)}, u32[]{:S(2)}) collective-permute-start(bf16[2,64,4,128]{3,1,2,0:T(8,128)(2,1)S(1)} %get-tuple-element.204), channel_id=1, source_target_pairs={{0,8},{8,16},{16,24},{1,9},{9,17},{17,25},{2,10},{10,18},{18,26},{... | collective-permute-start | bytes 393224 | tf_op jit(solution)/shard_map/ppermute | solution.py:19
  82.3 19.6 %collective-permute-start.12 = (bf16[2,64,4,128]{3,1,2,0:T(8,128)(2,1)S(1)}, bf16[2,64,4,128]{3,1,2,0:T(8,128)(2,1)S(1)}, u32[]{:S(2)}, u32[]{:S(2)}) collective-permute-start(bf16[2,64,4,128]{3,1,2,0:T(8,128)(2,1)S(1)} %get-tuple-element.205), channel_id=1, source_target_pairs={{8,0},{16,8},{24,16},{9,1},{17,9},{25,17},{10,2},{18,10},{26,18},{... | collective-permute-start | bytes 393224 | tf_op jit(solution)/shard_map/ppermute | solution.py:22
  105.5 12.1 %copy-start.1 = (bf16[2,64,64,128]{3,1,2,0:T(8,128)(2,1)S(1)}, bf16[2,64,64,128]{3,1,2,0:T(8,128)(2,1)}, u32[]{:S(2)}) copy-start(bf16[2,64,64,128]{3,1,2,0:T(8,128)(2,1)} %copy-done) | copy-start | bytes 6291460
  109.7 13.3 %collective-permute-start.13 = (bf16[2,64,72,4]{2,1,3,0:T(8,128)(2,1)S(1)}, bf16[2,64,72,4]{2,1,3,0:T(8,128)(2,1)S(1)}, u32[]{:S(2)}, u32[]{:S(2)}) collective-permute-start(bf16[2,64,72,4]{2,1,3,0:T(8,128)(2,1)S(1)} %copy.74), channel_id=1, source_target_pairs={{0,1},{1,2},{2,3},{3,4},{4,5},{5,6},{6,7},{8,9},{9,10},{10,11},{11... | collective-permute-start | bytes 221192 | tf_op jit(solution)/shard_map/ppermute | solution.py:19
  116.3 11.4 %collective-permute-start.14 = (bf16[2,64,72,4]{2,1,3,0:T(8,128)(2,1)S(1)}, bf16[2,64,72,4]{2,1,3,0:T(8,128)(2,1)S(1)}, u32[]{:S(2)}, u32[]{:S(2)}) collective-permute-start(bf16[2,64,72,4]{2,1,3,0:T(8,128)(2,1)S(1)} %copy.76), channel_id=1, source_target_pairs={{1,0},{2,1},{3,2},{4,3},{5,4},{6,5},{7,6},{9,8},{10,9},{11,10},{12... | collective-permute-start | bytes 221192 | tf_op jit(solution)/shard_map/ppermute | solution.py:22
  138.4 8.9 %copy-start.9 = (bf16[2,64,72,132]{3,1,2,0:T(8,128)(2,1)}, bf16[2,64,72,132]{3,1,2,0:T(8,128)(2,1)S(1)}, u32[]{:S(2)}) copy-start(bf16[2,64,72,132]{3,1,2,0:T(8,128)(2,1)S(1)} %get-tuple-element.196) | copy-start | bytes 7299076
  150.1 4.3 copy-start.12
  171.7 8.2 %copy-start.15 = (s32[2,8,1]{1,2,0:T(1,128)S(1)}, s32[2,8,1]{1,2,0:T(1,128)}, u32[]{:S(2)}) copy-start(s32[2,8,1]{1,2,0:T(1,128)} %param.9) | copy-start | bytes 196
  173.3 74.2 %all-to-all-start = ((bf16[2,64,64,128]{3,1,0,2:T(8,128)(2,1)}), bf16[2,64,64,128]{3,1,0,2:T(8,128)(2,1)S(1)}, u32[]{:S(2)}, u32[]{:S(2)}) async-start(bf16[2,64,64,128]{3,1,0,2:T(8,128)(2,1)} %copy.78), calls=%async_computation | async-start | bytes 4194304 | tf_op jit(solution)/shard_map/all_to_all | solution.py:91
  179.9 38.3 %collective-permute-start = (s32[2,8,1]{1,2,0:T(1,128)S(1)}, s32[2,8,1]{1,2,0:T(1,128)S(1)}, u32[]{:S(2)}, u32[]{:S(2)}) collective-permute-start(s32[2,8,1]{1,2,0:T(1,128)S(1)} %copy-done.15), channel_id=1, source_target_pairs={{0,1},{1,2},{2,3},{3,4},{4,5},{5,6},{6,7},{7,0},{8,9},{9,10},{10,1... | collective-permute-start | bytes 200 | tf_op jit(solution)/shard_map/ppermute | solution.py:96
  218.2 4.8 collective-permute-start.1
  223.0 4.8 collective-permute-start.2
  227.8 4.8 collective-permute-start.3
  232.6 4.8 collective-permute-start.4
  237.4 4.8 collective-permute-start.5
  242.2 5.0 collective-permute-start.6
  253.1 5.1 %copy-start.2 = (f32[64,64,128]{2,0,1:T(8,128)S(1)}, f32[64,64,128]{2,0,1:T(8,128)}, u32[]{:S(2)}) copy-start(f32[64,64,128]{2,0,1:T(8,128)} %get-tuple-element.291) | copy-start | bytes 6291460 | tf_op jit(solution)/shard_map/while
  264.5 5.1 %copy-start.2 = (f32[64,64,128]{2,0,1:T(8,128)S(1)}, f32[64,64,128]{2,0,1:T(8,128)}, u32[]{:S(2)}) copy-start(f32[64,64,128]{2,0,1:T(8,128)} %get-tuple-element.291) | copy-start | bytes 6291460 | tf_op jit(solution)/shard_map/while
  275.8 5.1 %copy-start.2 = (f32[64,64,128]{2,0,1:T(8,128)S(1)}, f32[64,64,128]{2,0,1:T(8,128)}, u32[]{:S(2)}) copy-start(f32[64,64,128]{2,0,1:T(8,128)} %get-tuple-element.291) | copy-start | bytes 6291460 | tf_op jit(solution)/shard_map/while
  287.1 5.1 %copy-start.2 = (f32[64,64,128]{2,0,1:T(8,128)S(1)}, f32[64,64,128]{2,0,1:T(8,128)}, u32[]{:S(2)}) copy-start(f32[64,64,128]{2,0,1:T(8,128)} %get-tuple-element.291) | copy-start | bytes 6291460 | tf_op jit(solution)/shard_map/while
  298.5 5.1 %copy-start.2 = (f32[64,64,128]{2,0,1:T(8,128)S(1)}, f32[64,64,128]{2,0,1:T(8,128)}, u32[]{:S(2)}) copy-start(f32[64,64,128]{2,0,1:T(8,128)} %get-tuple-element.291) | copy-start | bytes 6291460 | tf_op jit(solution)/shard_map/while
  309.8 5.1 %copy-start.2 = (f32[64,64,128]{2,0,1:T(8,128)S(1)}, f32[64,64,128]{2,0,1:T(8,128)}, u32[]{:S(2)}) copy-start(f32[64,64,128]{2,0,1:T(8,128)} %get-tuple-element.291) | copy-start | bytes 6291460 | tf_op jit(solution)/shard_map/while
  321.1 5.1 %copy-start.2 = (f32[64,64,128]{2,0,1:T(8,128)S(1)}, f32[64,64,128]{2,0,1:T(8,128)}, u32[]{:S(2)}) copy-start(f32[64,64,128]{2,0,1:T(8,128)} %get-tuple-element.291) | copy-start | bytes 6291460 | tf_op jit(solution)/shard_map/while
  332.5 5.1 %copy-start.2 = (f32[64,64,128]{2,0,1:T(8,128)S(1)}, f32[64,64,128]{2,0,1:T(8,128)}, u32[]{:S(2)}) copy-start(f32[64,64,128]{2,0,1:T(8,128)} %get-tuple-element.291) | copy-start | bytes 6291460 | tf_op jit(solution)/shard_map/while
  343.8 5.1 %copy-start.2 = (f32[64,64,128]{2,0,1:T(8,128)S(1)}, f32[64,64,128]{2,0,1:T(8,128)}, u32[]{:S(2)}) copy-start(f32[64,64,128]{2,0,1:T(8,128)} %get-tuple-element.291) | copy-start | bytes 6291460 | tf_op jit(solution)/shard_map/while
  355.1 5.1 %copy-start.2 = (f32[64,64,128]{2,0,1:T(8,128)S(1)}, f32[64,64,128]{2,0,1:T(8,128)}, u32[]{:S(2)}) copy-start(f32[64,64,128]{2,0,1:T(8,128)} %get-tuple-element.291) | copy-start | bytes 6291460 | tf_op jit(solution)/shard_map/while
  366.5 5.1 %copy-start.2 = (f32[64,64,128]{2,0,1:T(8,128)S(1)}, f32[64,64,128]{2,0,1:T(8,128)}, u32[]{:S(2)}) copy-start(f32[64,64,128]{2,0,1:T(8,128)} %get-tuple-element.291) | copy-start | bytes 6291460 | tf_op jit(solution)/shard_map/while
  377.8 5.1 %copy-start.2 = (f32[64,64,128]{2,0,1:T(8,128)S(1)}, f32[64,64,128]{2,0,1:T(8,128)}, u32[]{:S(2)}) copy-start(f32[64,64,128]{2,0,1:T(8,128)} %get-tuple-element.291) | copy-start | bytes 6291460 | tf_op jit(solution)/shard_map/while
  389.1 5.1 %copy-start.2 = (f32[64,64,128]{2,0,1:T(8,128)S(1)}, f32[64,64,128]{2,0,1:T(8,128)}, u32[]{:S(2)}) copy-start(f32[64,64,128]{2,0,1:T(8,128)} %get-tuple-element.291) | copy-start | bytes 6291460 | tf_op jit(solution)/shard_map/while
  400.5 5.1 %copy-start.2 = (f32[64,64,128]{2,0,1:T(8,128)S(1)}, f32[64,64,128]{2,0,1:T(8,128)}, u32[]{:S(2)}) copy-start(f32[64,64,128]{2,0,1:T(8,128)} %get-tuple-element.291) | copy-start | bytes 6291460 | tf_op jit(solution)/shard_map/while
  411.8 5.1 %copy-start.2 = (f32[64,64,128]{2,0,1:T(8,128)S(1)}, f32[64,64,128]{2,0,1:T(8,128)}, u32[]{:S(2)}) copy-start(f32[64,64,128]{2,0,1:T(8,128)} %get-tuple-element.291) | copy-start | bytes 6291460 | tf_op jit(solution)/shard_map/while
  423.1 5.1 %copy-start.2 = (f32[64,64,128]{2,0,1:T(8,128)S(1)}, f32[64,64,128]{2,0,1:T(8,128)}, u32[]{:S(2)}) copy-start(f32[64,64,128]{2,0,1:T(8,128)} %get-tuple-element.291) | copy-start | bytes 6291460 | tf_op jit(solution)/shard_map/while
  434.5 5.1 %copy-start.2 = (f32[64,64,128]{2,0,1:T(8,128)S(1)}, f32[64,64,128]{2,0,1:T(8,128)}, u32[]{:S(2)}) copy-start(f32[64,64,128]{2,0,1:T(8,128)} %get-tuple-element.291) | copy-start | bytes 6291460 | tf_op jit(solution)/shard_map/while
  445.8 5.1 %copy-start.2 = (f32[64,64,128]{2,0,1:T(8,128)S(1)}, f32[64,64,128]{2,0,1:T(8,128)}, u32[]{:S(2)}) copy-start(f32[64,64,128]{2,0,1:T(8,128)} %get-tuple-element.291) | copy-start | bytes 6291460 | tf_op jit(solution)/shard_map/while
  456.0 11.3 %all-to-all-start.2 = ((f32[8,8,128]{2,0,1:T(8,128)}), f32[8,8,128]{2,0,1:T(8,128)S(1)}, u32[]{:S(2)}, u32[]{:S(2)}) async-start(f32[8,8,128]{2,0,1:T(8,128)} %copy.84), calls=%async_computation.2 | async-start | bytes 65536 | tf_op jit(solution)/shard_map/all_to_all | solution.py:130
  467.3 31.6 %all-to-all-start.1 = ((bf16[8,2,32768]{2,1,0:T(2,128)(2,1)}), bf16[8,2,32768]{2,1,0:T(2,128)(2,1)S(1)}, u32[]{:S(2)}, u32[]{:S(2)}) async-start(bf16[8,2,32768]{2,1,0:T(2,128)(2,1)} %reshape.93), calls=%async_computation.1 | async-start | bytes 2097152 | tf_op jit(solution)/shard_map/all_to_all | solution.py:129
  (20 other events, 30.5 us)
